TPU v7x, 32 devices: a whole 2x2x4 slice. The times are simulated.
32 devices in a mesh: dp: 8 (over z, x), tensor: 4 (over y, core).
Axes of the slice: x: 2, y: 2, z: 4, core: 2. Of those that a mesh axis runs over, the one named last changes fastest.
Arguments:
- hidden_in: bfloat16 [8192, 768], P('dp'), may hold values from -6 to 6
- w_qkv: bfloat16 [3, 768, 768], P(None, None, 'tensor'), may hold values from -0.21875 to 0.21875
- w_out: bfloat16 [768, 768], P('tensor'), may hold values from -0.625 to 0.625
- w_ff1: bfloat16 [768, 768], P(None, 'tensor'), may hold values from -0.21875 to 0.21875
- w_ff2: bfloat16 [768, 768], P('tensor'), may hold values from -0.21875 to 0.21875
- ln1_gain: float32 [768], replicated, may hold values from 0.5 to 1.5
- ln1_bias: float32 [768], replicated, may hold values from -3 to 3
- ln2_gain: float32 [768], replicated, may hold values from 0.5 to 1.5
- ln2_bias: float32 [768], replicated, may hold values from -3 to 3
- spd_table: float32 [32, 32], P(None, 'tensor'), may hold values from -3 to 3
- edge_table: float32 [32, 32], P(None, 'tensor'), may hold values from -3 to 3
- kernel_w1: bfloat16 [128, 128], replicated, may hold values from -0.5 to 0.5
- kernel_w2: bfloat16 [128, 32], P(None, 'tensor'), may hold values from -0.5 to 0.5
- centers: float32 [128], replicated, may hold values from 0 to 8
- widths: float32 [128], replicated, may hold values from 0.3 to 3
- atom_count: int32 [128], P('dp'), may hold values from 16 to 64, as said below
- mol_mode: int32 [128], P('dp'), may hold values from 0 to 2
- spd_bucket: int32 [128, 64, 64], P('dp'), may hold values from 0 to 31
- edge_type: int32 [128, 64, 64], P('dp'), may hold values from 0 to 31
- dist_bucket: int32 [128, 64, 64], P('dp'), may hold values from 0 to 127
- cotangent: bfloat16 [8192, 768], P('dp'), may hold values from -6 to 6
Outputs:
- layer_out: bfloat16 [8192, 768], P('dp')
- grad_in: bfloat16 [8192, 768], P('dp')
- grad_qkv: float32 [3, 768, 768], P(None, None, 'tensor')
- grad_out: float32 [768, 768], P('tensor')
- grad_ff1: float32 [768, 768], P(None, 'tensor')
- grad_ff2: float32 [768, 768], P('tensor')
- grad_ln1_gain: float32 [768], replicated
- grad_ln1_bias: float32 [768], replicated
- grad_ln2_gain: float32 [768], replicated
- grad_ln2_bias: float32 [768], replicated
- grad_spd: float32 [32, 32], P(None, 'tensor')
- grad_edge: float32 [32, 32], P(None, 'tensor')
- grad_kernel_w1: float32 [128, 128], replicated
- grad_kernel_w2: float32 [128, 32], P(None, 'tensor')
- grad_centers: float32 [128], replicated
- grad_widths: float32 [128], replicated
Inputs may be any that keep to these rules, and one draw needn't show every extreme that they name: `atom_count`: every molecule has at least 16 real atoms, and some molecule has exactly 64.
All inputs are finite; a program needn't handle non-finite values.
Results may differ from a plain program's by a relative error of at most 0.02.
Values may be sent and summed in bfloat16 or wider, within the bound.
No kernel may reach another device: no remote copies, remote signals or barrier semaphores. Data moves between devices by JAX's collectives and lax.ppermute only.
A program may use at most 128 MiB of HBM per device.

v0:
```python
from functools import partial
import math
import jax
import jax.numpy as jnp
from jax import lax
from jax.sharding import PartitionSpec as P

DIST = 128
eps = 1e-05
neg_fill = -1000000000.0
highest = lax.Precision.HIGHEST


def norm_rows(values, gain, shift):
    center = values - jnp.mean(values, axis=-1, keepdims=True)
    spread = jnp.mean(center * center, axis=-1, keepdims=True)
    return center * lax.rsqrt(spread + eps) * gain + shift


def gelu_exact(values):
    return jax.nn.gelu(values, approximate=False)


def kernels(dist, centers, widths):
    place = dist.astype(jnp.float32)[..., None] * (8.0 / DIST)
    offset = (place - centers) / widths
    return jnp.exp(-0.5 * offset * offset) / widths


def kernel_geo(weights, dist_rows):
    kernel_w1, kernel_w2, centers, widths = weights
    total = dist_rows.shape[0]
    block = math.gcd(total, 16384)

    def one_block(rows):
        basis = kernels(rows, centers, widths).astype(jnp.bfloat16)
        inner = jnp.dot(basis, kernel_w1, preferred_element_type=jnp.float32)
        hidden = gelu_exact(inner).astype(jnp.bfloat16)
        return jnp.dot(hidden, kernel_w2, preferred_element_type=jnp.float32)

    result = lax.map(one_block, dist_rows.reshape(total // block, block))
    return result.reshape(total, kernel_w2.shape[1])


def kernel_grads(weights, dist_rows, grad_geo):
    kernel_w1, kernel_w2, centers, widths = weights
    total = dist_rows.shape[0]
    block = math.gcd(total, 16384)

    def one_block(carry, items):
        acc_one, acc_two, acc_center, acc_width = carry
        rows, grad_rows = items
        basis, basis_pull = jax.vjp(lambda cen, wid: kernels(rows, cen, wid), centers, widths)
        basis_b = basis.astype(jnp.bfloat16)
        inner = jnp.dot(basis_b, kernel_w1, preferred_element_type=jnp.float32)
        hidden, gelu_pull = jax.vjp(gelu_exact, inner)
        hidden_b = hidden.astype(jnp.bfloat16)
        acc_two = acc_two + jnp.dot(hidden_b.T, grad_rows, preferred_element_type=jnp.float32)
        grad_hidden = jnp.dot(grad_rows, kernel_w2.T, preferred_element_type=jnp.float32)
        grad_inner = gelu_pull(grad_hidden)[0].astype(jnp.bfloat16)
        acc_one = acc_one + jnp.dot(basis_b.T, grad_inner, preferred_element_type=jnp.float32)
        grad_basis = jnp.dot(grad_inner, kernel_w1.T, preferred_element_type=jnp.float32)
        grad_center, grad_width = basis_pull(grad_basis)
        return ((acc_one, acc_two, acc_center + grad_center, acc_width + grad_width), None)

    start_carry = (
        jnp.zeros(kernel_w1.shape, jnp.float32),
        jnp.zeros(kernel_w2.shape, jnp.float32),
        jnp.zeros(centers.shape, jnp.float32),
        jnp.zeros(widths.shape, jnp.float32),
    )
    result, unused = lax.scan(
        one_block,
        start_carry,
        (
            dist_rows.reshape(total // block, block),
            grad_geo.reshape(total // block, block, grad_geo.shape[1]),
        ),
    )
    return result


def block_bias(tables, mode, spd_ids, edge_ids, geo):
    spd_table, edge_table = tables
    spd_hot = jax.nn.one_hot(spd_ids, spd_table.shape[0], dtype=jnp.float32)
    edge_hot = jax.nn.one_hot(edge_ids, edge_table.shape[0], dtype=jnp.float32)
    flat = jnp.dot(spd_hot, spd_table, precision=highest) + jnp.dot(
        edge_hot, edge_table, precision=highest
    )
    two_flag = (mode != 1).astype(jnp.float32)[:, None, None, None]
    three_flag = (mode != 0).astype(jnp.float32)[:, None, None, None]
    return (two_flag * flat + three_flag * geo, spd_hot, edge_hot, two_flag, three_flag)


def scores_of(query, keyset, bias, count):
    atoms = query.shape[1]
    scores = jnp.einsum("bihe,bjhe->bhij", query, keyset, preferred_element_type=jnp.float32)
    scores = scores + jnp.transpose(bias, (0, 3, 1, 2))
    keep = (jnp.arange(atoms)[None, :] < count[:, None])[:, None, None, :]
    return jnp.where(keep, scores, neg_fill)


def attend(tables, items):
    query, keyset, values, count, mode, spd_ids, edge_ids, geo = items
    bias = block_bias(tables, mode, spd_ids, edge_ids, geo)[0]
    scores = scores_of(query, keyset, bias, count)
    row_max = jnp.max(scores, axis=-1, keepdims=True)
    expos = jnp.exp(scores - row_max)
    totals = jnp.sum(expos, axis=-1, keepdims=True)
    probs = (expos / totals).astype(jnp.bfloat16)
    mixed = jnp.einsum("bhij,bjhe->bihe", probs, values, preferred_element_type=jnp.float32)
    return (mixed.astype(jnp.bfloat16), row_max + jnp.log(totals))


def attend_back(tables, carry, items):
    query, keyset, values, grad_mixed, log_sums, count, mode, spd_ids, edge_ids, geo = items
    acc_spd, acc_edge = carry
    bias, spd_hot, edge_hot, two_flag, three_flag = block_bias(tables, mode, spd_ids, edge_ids, geo)
    scores = scores_of(query, keyset, bias, count)
    probs = jnp.exp(scores - log_sums)
    grad_values = jnp.einsum(
        "bhij,bihe->bjhe",
        probs.astype(jnp.bfloat16),
        grad_mixed,
        preferred_element_type=jnp.float32,
    )
    grad_probs = jnp.einsum(
        "bihe,bjhe->bhij", grad_mixed, values, preferred_element_type=jnp.float32
    )
    grad_scores = probs * (grad_probs - jnp.sum(probs * grad_probs, axis=-1, keepdims=True))
    grad_scores = grad_scores.astype(jnp.bfloat16)
    grad_query = jnp.einsum(
        "bhij,bjhe->bihe", grad_scores, keyset, preferred_element_type=jnp.float32
    )
    grad_keys = jnp.einsum(
        "bhij,bihe->bjhe", grad_scores, query, preferred_element_type=jnp.float32
    )
    grad_bias = jnp.transpose(grad_scores, (0, 2, 3, 1))
    flat_grad = two_flag.astype(jnp.bfloat16) * grad_bias
    acc_spd = acc_spd + jnp.einsum(
        "bijs,bijh->sh", spd_hot.astype(jnp.bfloat16), flat_grad, preferred_element_type=jnp.float32
    )
    acc_edge = acc_edge + jnp.einsum(
        "bijs,bijh->sh",
        edge_hot.astype(jnp.bfloat16),
        flat_grad,
        preferred_element_type=jnp.float32,
    )
    geo_grad = three_flag.astype(jnp.bfloat16) * grad_bias
    outputs = (
        grad_query.astype(jnp.bfloat16),
        grad_keys.astype(jnp.bfloat16),
        grad_values.astype(jnp.bfloat16),
        geo_grad,
    )
    return ((acc_spd, acc_edge), outputs)


def gain_grads(values, gain, shift, grad_rows):
    pull = jax.vjp(norm_rows, values, gain, shift)[1]
    return pull(grad_rows)


def body(
    hidden_in,
    w_qkv,
    w_out,
    w_ff1,
    w_ff2,
    ln1_gain,
    ln1_bias,
    ln2_gain,
    ln2_bias,
    spd_table,
    edge_table,
    kernel_w1,
    kernel_w2,
    centers,
    widths,
    atom_count,
    mol_mode,
    spd_bucket,
    edge_type,
    dist_bucket,
    cotangent,
):
    tokens = hidden_in.shape[0]
    mols, atoms = (spd_bucket.shape[0], spd_bucket.shape[1])
    heads_here = spd_table.shape[1]
    columns = w_qkv.shape[2]
    head_dim = columns // heads_here
    group = math.gcd(mols, max(1, 2048 // atoms))
    count_blocks = mols // group
    scale = 1.0 / math.sqrt(head_dim)
    tables = (spd_table, edge_table)
    pairs = mols * atoms * atoms
    dist_rows = dist_bucket.reshape(pairs)

    def by_block(array):
        return array.reshape((count_blocks, group) + array.shape[1:])

    def heads_view(array):
        return array.reshape(count_blocks, group, atoms, heads_here, head_dim)

    source = hidden_in.astype(jnp.float32)
    upstream = cotangent.astype(jnp.float32)
    share_rows = tokens // lax.axis_size("tensor")
    start = lax.axis_index("tensor") * share_rows
    source_share = lax.dynamic_slice_in_dim(source, start, share_rows, 0)
    geo = kernel_geo((kernel_w1, kernel_w2, centers, widths), dist_rows)
    geo_view = geo.reshape(count_blocks, group, atoms, atoms, heads_here)
    normed_one = norm_rows(source, ln1_gain, ln1_bias).astype(jnp.bfloat16)
    projected = jnp.einsum("td,kdc->ktc", normed_one, w_qkv, preferred_element_type=jnp.float32)
    query_b = (projected[0] * scale).astype(jnp.bfloat16)
    key_b = projected[1].astype(jnp.bfloat16)
    value_b = projected[2].astype(jnp.bfloat16)
    int_items = (
        by_block(atom_count),
        by_block(mol_mode),
        by_block(spd_bucket),
        by_block(edge_type),
        geo_view,
    )
    attended, log_sums = lax.map(
        partial(attend, tables),
        (heads_view(query_b), heads_view(key_b), heads_view(value_b)) + int_items,
    )
    attended = attended.reshape(tokens, columns)
    attn_part = jnp.dot(attended, w_out, preferred_element_type=jnp.float32)
    middle = source + lax.psum(attn_part.astype(jnp.bfloat16), "tensor").astype(jnp.float32)
    normed_two = norm_rows(middle, ln2_gain, ln2_bias).astype(jnp.bfloat16)
    inner = jnp.dot(normed_two, w_ff1, preferred_element_type=jnp.float32)
    active = gelu_exact(inner).astype(jnp.bfloat16)
    ffn_part = jnp.dot(active, w_ff2, preferred_element_type=jnp.float32)
    layer_out = (
        middle + lax.psum(ffn_part.astype(jnp.bfloat16), "tensor").astype(jnp.float32)
    ).astype(jnp.bfloat16)
    grad_ff2 = jnp.dot(active.T, cotangent, preferred_element_type=jnp.float32)
    grad_active = jnp.dot(cotangent, w_ff2.T, preferred_element_type=jnp.float32)
    gelu_pull = jax.vjp(gelu_exact, inner)[1]
    grad_inner = gelu_pull(grad_active)[0].astype(jnp.bfloat16)
    grad_ff1 = jnp.dot(normed_two.T, grad_inner, preferred_element_type=jnp.float32)
    two_part = jnp.dot(grad_inner, w_ff1.T, preferred_element_type=jnp.float32)
    two_grad = lax.psum(two_part.astype(jnp.bfloat16), "tensor").astype(jnp.float32)
    back_middle = gain_grads(middle, ln2_gain, ln2_bias, two_grad)[0]
    middle_share = lax.dynamic_slice_in_dim(middle, start, share_rows, 0)
    two_share = lax.dynamic_slice_in_dim(two_grad, start, share_rows, 0)
    unused, grad_g2, grad_b2 = gain_grads(middle_share, ln2_gain, ln2_bias, two_share)
    middle_grad = upstream + back_middle
    middle_grad_b = middle_grad.astype(jnp.bfloat16)
    grad_out = jnp.dot(attended.T, middle_grad_b, preferred_element_type=jnp.float32)
    grad_attended = jnp.dot(middle_grad_b, w_out.T, preferred_element_type=jnp.float32).astype(
        jnp.bfloat16
    )
    carry_start = (
        jnp.zeros(spd_table.shape, jnp.float32),
        jnp.zeros(edge_table.shape, jnp.float32),
    )
    table_grads, back_outs = lax.scan(
        partial(attend_back, tables),
        carry_start,
        (
            heads_view(query_b),
            heads_view(key_b),
            heads_view(value_b),
            heads_view(grad_attended),
            log_sums,
        )
        + int_items,
    )
    grad_spd, grad_edge = table_grads
    geo_grad = back_outs[3].reshape(pairs, heads_here)
    grad_kw1, grad_kw2, grad_cen, grad_wid = kernel_grads(
        (kernel_w1, kernel_w2, centers, widths), dist_rows, geo_grad
    )
    grad_qkv_b = jnp.stack(
        [
            back_outs[0].reshape(tokens, columns),
            back_outs[1].reshape(tokens, columns),
            back_outs[2].reshape(tokens, columns),
        ]
    )
    factor = jnp.array([scale, 1.0, 1.0], jnp.float32)[:, None, None]
    grad_qkv = (
        jnp.einsum("td,ktc->kdc", normed_one, grad_qkv_b, preferred_element_type=jnp.float32)
        * factor
    )
    one_parts = jnp.einsum("ktc,kdc->ktd", grad_qkv_b, w_qkv, preferred_element_type=jnp.float32)
    one_part = jnp.sum(one_parts * factor, axis=0)
    one_grad = lax.psum(one_part.astype(jnp.bfloat16), "tensor").astype(jnp.float32)
    back_source = gain_grads(source, ln1_gain, ln1_bias, one_grad)[0]
    one_share = lax.dynamic_slice_in_dim(one_grad, start, share_rows, 0)
    unused, grad_g1, grad_b1 = gain_grads(source_share, ln1_gain, ln1_bias, one_share)
    grad_in = (middle_grad + back_source).astype(jnp.bfloat16)
    sharded = (
        lax.psum(grad_qkv.astype(jnp.bfloat16), "dp").astype(jnp.float32),
        lax.psum(grad_out.astype(jnp.bfloat16), "dp").astype(jnp.float32),
        lax.psum(grad_ff1.astype(jnp.bfloat16), "dp").astype(jnp.float32),
        lax.psum(grad_ff2.astype(jnp.bfloat16), "dp").astype(jnp.float32),
        lax.psum(grad_spd.astype(jnp.bfloat16), "dp").astype(jnp.float32),
        lax.psum(grad_edge.astype(jnp.bfloat16), "dp").astype(jnp.float32),
        lax.psum(grad_kw2.astype(jnp.bfloat16), "dp").astype(jnp.float32),
    )
    shared = lax.psum(
        (grad_kw1, grad_cen, grad_wid, grad_g1, grad_b1, grad_g2, grad_b2), ("dp", "tensor")
    )
    return (
        layer_out,
        grad_in,
        sharded[0],
        sharded[1],
        sharded[2],
        sharded[3],
        shared[3],
        shared[4],
        shared[5],
        shared[6],
        sharded[4],
        sharded[5],
        shared[0],
        sharded[6],
        shared[1],
        shared[2],
    )


def solution(mesh):
    in_specs = (
        P("dp", None),
        P(None, None, "tensor"),
        P("tensor", None),
        P(None, "tensor"),
        P("tensor", None),
        P(),
        P(),
        P(),
        P(),
        P(None, "tensor"),
        P(None, "tensor"),
        P(),
        P(None, "tensor"),
        P(),
        P(),
        P("dp"),
        P("dp"),
        P("dp", None, None),
        P("dp", None, None),
        P("dp", None, None),
        P("dp", None),
    )
    out_specs = (
        P("dp", None),
        P("dp", None),
        P(None, None, "tensor"),
        P("tensor", None),
        P(None, "tensor"),
        P("tensor", None),
        P(),
        P(),
        P(),
        P(),
        P(None, "tensor"),
        P(None, "tensor"),
        P(),
        P(None, "tensor"),
        P(),
        P(),
    )
    return jax.shard_map(body, mesh=mesh, in_specs=in_specs, out_specs=out_specs, check_vma=False)
```

profile of v0, /device:TPU:1, one launch (start us, length us, event | category | flops | bytes accessed | tf_op | source)
XLA Modules:
  0.0 702.5 jit_solution(9813940309770022953)
XLA Ops:
  17.9 129.2 %while.6 = (s32[]{:T(128)}, f32[4,16384,8]{1,0,2:T(4,128)}, s32[4,16384]{1,0:T(4,128)S(1)}, f32[128]{0:T(128)S(1)}, f32[128]{0:T(128)S(1)}, /*index=5*/bf16[128,...) while((s32[]{:T(128)}, f32[4,16384,8]{1,0,2:T(4,128)}, s32[4,16384]{1,0:T(4,128)S(1)}, ...), condition=%wide.region_3.4_spmd, body=%wide.region_2.3_spmd.sunk | while | flops 719355904 | bytes 2853997 | solution.py:41
  18.2 21.2 %convolution_bitcast_fusion.2 = f32[1,16384,8]{1,2,0:T(8,128)S(1)} fusion(bf16[128,8]{0,1:T(8,128)(2,1)S(1)} %get-tuple-element.560, bf16[128,128]{1,0:T(8,128)(2,1)S(1)} %get-tuple-element.559, f32[128]{0:T(128)S(1)} %get-tuple-element.558, f32[128]{0:T(128)S(1)} %get-tuple-element.557, f32[16384]{0:T(1024)S(1)} %bitcast.180), kind=kOutput, calls=%fused_computation.clone.1 | convolution fusion | flops 719323136 | bytes 625664 | tf_op jit(solution)/shard_map/while/body/eval_jaxpr/dot_general | solution.py:39
  39.9 10.5 %dynamic_update_slice.20 = f32[4,16384,8]{1,0,2:T(4,128)} dynamic-update-slice(f32[4,16384,8]{1,0,2:T(4,128)} %get-tuple-element.546, f32[1,16384,8]{1,0,2:T(1,128)S(1)} %copy.132, s32[]{:T(128)S(6)} %copy.136, s32[]{:T(128)} %constant.311.clone.1..sunk, s32[]{:T(128)} %constant.311.clone.1..sunk) | dynamic-update-slice | bytes 1048580 | tf_op jit(solution)/shard_map/while/body/jit(dynamic_update_index_in_dim)/dynamic_update_slice | solution.py:41
  50.4 21.2 %convolution_bitcast_fusion.2 = f32[1,16384,8]{1,2,0:T(8,128)S(1)} fusion(bf16[128,8]{0,1:T(8,128)(2,1)S(1)} %get-tuple-element.560, bf16[128,128]{1,0:T(8,128)(2,1)S(1)} %get-tuple-element.559, f32[128]{0:T(128)S(1)} %get-tuple-element.558, f32[128]{0:T(128)S(1)} %get-tuple-element.557, f32[16384]{0:T(1024)S(1)} %bitcast.180), kind=kOutput, calls=%fused_computation.clone.1 | convolution fusion | flops 719323136 | bytes 625664 | tf_op jit(solution)/shard_map/while/body/eval_jaxpr/dot_general | solution.py:39
  72.2 10.5 %dynamic_update_slice.20 = f32[4,16384,8]{1,0,2:T(4,128)} dynamic-update-slice(f32[4,16384,8]{1,0,2:T(4,128)} %get-tuple-element.546, f32[1,16384,8]{1,0,2:T(1,128)S(1)} %copy.132, s32[]{:T(128)S(6)} %copy.136, s32[]{:T(128)} %constant.311.clone.1..sunk, s32[]{:T(128)} %constant.311.clone.1..sunk) | dynamic-update-slice | bytes 1048580 | tf_op jit(solution)/shard_map/while/body/jit(dynamic_update_index_in_dim)/dynamic_update_slice | solution.py:41
  82.7 21.2 %convolution_bitcast_fusion.2 = f32[1,16384,8]{1,2,0:T(8,128)S(1)} fusion(bf16[128,8]{0,1:T(8,128)(2,1)S(1)} %get-tuple-element.560, bf16[128,128]{1,0:T(8,128)(2,1)S(1)} %get-tuple-element.559, f32[128]{0:T(128)S(1)} %get-tuple-element.558, f32[128]{0:T(128)S(1)} %get-tuple-element.557, f32[16384]{0:T(1024)S(1)} %bitcast.180), kind=kOutput, calls=%fused_computation.clone.1 | convolution fusion | flops 719323136 | bytes 625664 | tf_op jit(solution)/shard_map/while/body/eval_jaxpr/dot_general | solution.py:39
  104.4 10.5 %dynamic_update_slice.20 = f32[4,16384,8]{1,0,2:T(4,128)} dynamic-update-slice(f32[4,16384,8]{1,0,2:T(4,128)} %get-tuple-element.546, f32[1,16384,8]{1,0,2:T(1,128)S(1)} %copy.132, s32[]{:T(128)S(6)} %copy.136, s32[]{:T(128)} %constant.311.clone.1..sunk, s32[]{:T(128)} %constant.311.clone.1..sunk) | dynamic-update-slice | bytes 1048580 | tf_op jit(solution)/shard_map/while/body/jit(dynamic_update_index_in_dim)/dynamic_update_slice | solution.py:41
  115.0 21.2 %convolution_bitcast_fusion.2 = f32[1,16384,8]{1,2,0:T(8,128)S(1)} fusion(bf16[128,8]{0,1:T(8,128)(2,1)S(1)} %get-tuple-element.560, bf16[128,128]{1,0:T(8,128)(2,1)S(1)} %get-tuple-element.559, f32[128]{0:T(128)S(1)} %get-tuple-element.558, f32[128]{0:T(128)S(1)} %get-tuple-element.557, f32[16384]{0:T(1024)S(1)} %bitcast.180), kind=kOutput, calls=%fused_computation.clone.1 | convolution fusion | flops 719323136 | bytes 625664 | tf_op jit(solution)/shard_map/while/body/eval_jaxpr/dot_general | solution.py:39
  136.7 10.5 %dynamic_update_slice.20 = f32[4,16384,8]{1,0,2:T(4,128)} dynamic-update-slice(f32[4,16384,8]{1,0,2:T(4,128)} %get-tuple-element.546, f32[1,16384,8]{1,0,2:T(1,128)S(1)} %copy.132, s32[]{:T(128)S(6)} %copy.136, s32[]{:T(128)} %constant.311.clone.1..sunk, s32[]{:T(128)} %constant.311.clone.1..sunk) | dynamic-update-slice | bytes 1048580 | tf_op jit(solution)/shard_map/while/body/jit(dynamic_update_index_in_dim)/dynamic_update_slice | solution.py:41
  147.9 5.0 squeeze.56
  152.9 5.5 copy.59
  163.3 7.7 %fusion.83 = f32[16,64,64,8]{2,3,1,0:T(8,128)} fusion(s32[16,64,64]{2,1,0:T(8,128)} %param.43, f32[32,8]{0,1:T(8,128)S(1)} %copy-done.68), kind=kOutput, calls=%fused_computation.114 | convolution fusion | flops 203423744 | bytes 2360320 | tf_op jit(solution)/shard_map/while/body/eval_jaxpr/dot_general | solution.py:87
  171.0 5.4 copy.56
  176.4 7.5 %fusion.82 = f32[16,64,64,8]{2,3,1,0:T(8,128)} fusion(s32[16,64,64]{2,1,0:T(8,128)} %param.44, f32[32,8]{0,1:T(8,128)S(1)} %copy-done.69), kind=kOutput, calls=%fused_computation.112 | convolution fusion | flops 203423744 | bytes 2360320 | tf_op jit(solution)/shard_map/while/body/eval_jaxpr/dot_general | solution.py:87
  183.9 5.4 copy.57
  189.3 8.2 %fusion.153 = (f32[16,8,64]{2,1,0:T(8,128)S(1)}, f32[16,8,64,64]{2,3,1,0:T(8,128)S(1)}, f32[16,64,64,8]{1,2,3,0:T(8,128)}, f32[16,8,64,64]{2,3,1,0:T(8,128)}) fusion(pred[16,64]{1,0:T(8,128)(4,1)S(1)} %copy-done.61, f32[16,64,64,8]{1,2,3,0:T(8,128)} %copy.59, f32[16]{0:T(128)S(1)} %copy-done.75, f32[16,64,64,8]{1,2,3,0:T(8,128)} %copy.56, ...), kind=kOutput, calls=%fused_computation.248 | convolution fusion | flops 28827648 | bytes 13403264 | tf_op jit(solution)/shard_map/while/body/eval_jaxpr/bihe,bjhe->bhij/dot_general | solution.py:97
  211.7 39.8 %all-reduce.10.cloned.1.call-done = bf16[1024,768]{1,0:T(8,128)(2,1)} async-done(((bf16[1024,768]{1,0:T(8,128)(2,1)}), bf16[1024,768]{1,0:T(8,128)(2,1)}) %all-reduce.10.cloned.1.call-update) | async-done | bytes 1572880 | tf_op jit(solution)/shard_map/psum | solution.py:230
  274.6 36.9 %all-reduce.12.cloned.1.call-done = bf16[1024,768]{1,0:T(8,128)(2,1)} async-done(((bf16[1024,768]{1,0:T(8,128)(2,1)}), bf16[1024,768]{1,0:T(8,128)(2,1)}) %all-reduce.12.cloned.1.call-update) | async-done | bytes 1572880 | tf_op jit(solution)/shard_map/psum | solution.py:244
  353.1 6.6 broadcast_multiply_fusion.1
  375.6 165.0 %while.7 = (s32[]{:T(128)}, f32[128,128]{1,0:T(8,128)S(1)}, f32[128,8]{0,1:T(8,128)S(1)}, f32[128]{0:T(128)}, f32[128]{0:T(128)}, /*index=5*/s32[4,16384]{1,0:T(...) while((s32[]{:T(128)}, f32[128,128]{1,0:T(8,128)S(1)}, ...), condition=%wide.region_40.41_spmd.clone, body=%wide.region_36.40_spmd.clone.sunk | while | flops 1914768128 | bytes 101811056 | solution.py:72
  376.8 19.5 %fusion.218 = (f32[16384,128]{1,0:T(8,128)S(1)}, f32[16384,128]{1,0:T(8,128)S(1)}) fusion(bf16[128,128]{1,0:T(8,128)(2,1)S(1)} %get-tuple-element.599, f32[128]{0:T(128)S(1)} %get-tuple-element.598, f32[128]{0:T(128)S(1)} %get-tuple-element.597, f32[16384]{0:T(1024)S(1)} %bitcast.173), kind=kOutput, calls=%fused_computation.69.clone.1 | convolution fusion | flops 679477248 | bytes 16876544 | tf_op jit(solution)/shard_map/while/body/eval_jaxpr/dot_general | solution.py:55
  397.1 4.3 add_convert_fusion.9
  408.9 7.4 %fusion.222 = (f32[128]{0:T(128)S(1)}, f32[128]{0:T(128)S(1)}, f32[128]{0:T(128)S(1)}) fusion(f32[16384,128]{1,0:T(8,128)S(1)} %get-tuple-element.529, f32[128]{0:T(128)S(1)} %divide_bitcast_fusion.2, f32[128]{0:T(128)S(1)} %get-tuple-element.597, f32[16384]{0:T(1024)S(1)} %bitcast.176, f32[128]{0:T(128)S(1)} %get-tuple-element.598, ...), kind=kLoop, calls=%fused_computation.66.clone.1 | loop fusion | flops 25165440 | bytes 16845824 | tf_op jit(solution)/shard_map/while/body/eval_jaxpr/transpose(jvp())/reduce_sum | solution.py:26
  418.0 19.5 %fusion.218 = (f32[16384,128]{1,0:T(8,128)S(1)}, f32[16384,128]{1,0:T(8,128)S(1)}) fusion(bf16[128,128]{1,0:T(8,128)(2,1)S(1)} %get-tuple-element.599, f32[128]{0:T(128)S(1)} %get-tuple-element.598, f32[128]{0:T(128)S(1)} %get-tuple-element.597, f32[16384]{0:T(1024)S(1)} %bitcast.173), kind=kOutput, calls=%fused_computation.69.clone.1 | convolution fusion | flops 679477248 | bytes 16876544 | tf_op jit(solution)/shard_map/while/body/eval_jaxpr/dot_general | solution.py:55
  450.1 7.4 %fusion.222 = (f32[128]{0:T(128)S(1)}, f32[128]{0:T(128)S(1)}, f32[128]{0:T(128)S(1)}) fusion(f32[16384,128]{1,0:T(8,128)S(1)} %get-tuple-element.529, f32[128]{0:T(128)S(1)} %divide_bitcast_fusion.2, f32[128]{0:T(128)S(1)} %get-tuple-element.597, f32[16384]{0:T(1024)S(1)} %bitcast.176, f32[128]{0:T(128)S(1)} %get-tuple-element.598, ...), kind=kLoop, calls=%fused_computation.66.clone.1 | loop fusion | flops 25165440 | bytes 16845824 | tf_op jit(solution)/shard_map/while/body/eval_jaxpr/transpose(jvp())/reduce_sum | solution.py:26
  459.1 19.5 %fusion.218 = (f32[16384,128]{1,0:T(8,128)S(1)}, f32[16384,128]{1,0:T(8,128)S(1)}) fusion(bf16[128,128]{1,0:T(8,128)(2,1)S(1)} %get-tuple-element.599, f32[128]{0:T(128)S(1)} %get-tuple-element.598, f32[128]{0:T(128)S(1)} %get-tuple-element.597, f32[16384]{0:T(1024)S(1)} %bitcast.173), kind=kOutput, calls=%fused_computation.69.clone.1 | convolution fusion | flops 679477248 | bytes 16876544 | tf_op jit(solution)/shard_map/while/body/eval_jaxpr/dot_general | solution.py:55
  491.2 7.4 %fusion.222 = (f32[128]{0:T(128)S(1)}, f32[128]{0:T(128)S(1)}, f32[128]{0:T(128)S(1)}) fusion(f32[16384,128]{1,0:T(8,128)S(1)} %get-tuple-element.529, f32[128]{0:T(128)S(1)} %divide_bitcast_fusion.2, f32[128]{0:T(128)S(1)} %get-tuple-element.597, f32[16384]{0:T(1024)S(1)} %bitcast.176, f32[128]{0:T(128)S(1)} %get-tuple-element.598, ...), kind=kLoop, calls=%fused_computation.66.clone.1 | loop fusion | flops 25165440 | bytes 16845824 | tf_op jit(solution)/shard_map/while/body/eval_jaxpr/transpose(jvp())/reduce_sum | solution.py:26
  500.3 19.5 %fusion.218 = (f32[16384,128]{1,0:T(8,128)S(1)}, f32[16384,128]{1,0:T(8,128)S(1)}) fusion(bf16[128,128]{1,0:T(8,128)(2,1)S(1)} %get-tuple-element.599, f32[128]{0:T(128)S(1)} %get-tuple-element.598, f32[128]{0:T(128)S(1)} %get-tuple-element.597, f32[16384]{0:T(1024)S(1)} %bitcast.173), kind=kOutput, calls=%fused_computation.69.clone.1 | convolution fusion | flops 679477248 | bytes 16876544 | tf_op jit(solution)/shard_map/while/body/eval_jaxpr/dot_general | solution.py:55
  532.4 7.4 %fusion.222 = (f32[128]{0:T(128)S(1)}, f32[128]{0:T(128)S(1)}, f32[128]{0:T(128)S(1)}) fusion(f32[16384,128]{1,0:T(8,128)S(1)} %get-tuple-element.529, f32[128]{0:T(128)S(1)} %divide_bitcast_fusion.2, f32[128]{0:T(128)S(1)} %get-tuple-element.597, f32[16384]{0:T(1024)S(1)} %bitcast.176, f32[128]{0:T(128)S(1)} %get-tuple-element.598, ...), kind=kLoop, calls=%fused_computation.66.clone.1 | loop fusion | flops 25165440 | bytes 16845824 | tf_op jit(solution)/shard_map/while/body/eval_jaxpr/transpose(jvp())/reduce_sum | solution.py:26
  549.8 18.0 %all-reduce.1 = (bf16[32,8]{0,1:T(8,128)(2,1)S(1)}, bf16[32,8]{0,1:T(8,128)(2,1)S(1)}, bf16[128,8]{0,1:T(8,128)(2,1)S(1)}) all-reduce(bf16[32,8]{0,1:T(8,128)(2,1)S(1)} %fusion.122, bf16[32,8]{0,1:T(8,128)(2,1)S(1)} %fusion.123, bf16[128,8]{0,1:T(8,128)(2,1)S(1)} %convert_element_type.292), channel_id=1, replica_groups=mesh['dp'=8,'tensor'=4] {'dp'}, use_global_device_ids=true, to_apply=%region_34.35 | all-reduce | flops 1536 | bytes 6144 | tf_op jit(solution)/shard_map/psum | solution.py:300
  582.9 40.9 %all-reduce = (f32[768]{0:T(1024)}, f32[768]{0:T(1024)}, f32[768]{0:T(1024)}, f32[768]{0:T(1024)}, f32[128]{0:T(128)}, /*index=5*/f32[128]{0:T(128)}) all-reduce(f32[768]{0:T(1024)S(1)} %get-tuple-element.320, f32[768]{0:T(1024)S(1)} %get-tuple-element.319, ...), channel_id=1, replica_groups=mesh['dp'=8,'tensor'=4] {'dp','tensor'}, use_global_device_ids=true, to_apply=%region_25.26 | all-reduce | flops 3328 | bytes 26624 | tf_op jit(solution)/shard_map/psum | solution.py:304
  631.8 62.5 %all-reduce.14.cloned.1.call-done = f32[128,128]{1,0:T(8,128)} async-done(((f32[128,128]{1,0:T(8,128)}), f32[128,128]{1,0:T(8,128)}) %all-reduce.14.cloned.1.call-update) | async-done | bytes 65552 | tf_op jit(solution)/shard_map/psum | solution.py:304
  (359 shorter events, 198.9 us)
Async XLA Ops:
  7.2 244.3 %all-reduce.10.cloned.1.call-start = ((), (), s32[]{:S(2)}) async-start(), calls=%async_computation | async-start | bytes 3145728 | tf_op jit(solution)/shard_map/psum | solution.py:230
  159.7 39.1 %copy-start.26 = (bf16[16,64,8,24]{1,0,3,2:T(8,128)(2,1)}, bf16[16,64,8,24]{1,0,3,2:T(8,128)(2,1)S(1)}, u32[]{:S(2)}) copy-start(bf16[16,64,8,24]{1,0,3,2:T(8,128)(2,1)S(1)} %convert_element_type.239) | copy-start | bytes 1179652
  163.3 26.0 %copy-start.18 = (bf16[16,64,8,24]{1,0,3,2:T(8,128)(2,1)}, bf16[16,64,8,24]{1,0,3,2:T(8,128)(2,1)S(1)}, u32[]{:S(2)}) copy-start(bf16[16,64,8,24]{1,0,3,2:T(8,128)(2,1)S(1)} %convert_element_type.242) | copy-start | bytes 1179652
  206.6 105.0 %all-reduce.12.cloned.1.call-start = ((), (), s32[]{:S(2)}) async-start(), calls=%async_computation.1 | async-start | bytes 3145728 | tf_op jit(solution)/shard_map/psum | solution.py:244
  209.8 46.1 %copy-start.64 = (f32[256]{0:T(256)}, f32[256]{0:T(256)S(1)}, u32[]{:S(2)}) copy-start(f32[256]{0:T(256)S(1)} %broadcast_multiply_fusion.5) | copy-start | bytes 3076
  211.7 44.2 %copy-start.45 = (f32[768]{0:T(1024)S(1)}, f32[768]{0:T(1024)}, u32[]{:S(2)}) copy-start(f32[768]{0:T(1024)} %param.33) | copy-start | bytes 9220
  211.7 44.2 %copy-start.70 = (f32[768]{0:T(1024)S(1)}, f32[768]{0:T(1024)}, u32[]{:S(2)}) copy-start(f32[768]{0:T(1024)} %param.34) | copy-start | bytes 9220
  264.8 9.8 %copy-start.66 = (f32[256]{0:T(256)}, f32[256]{0:T(256)S(1)}, u32[]{:S(2)}) copy-start(f32[256]{0:T(256)S(1)} %broadcast_multiply_fusion.4) | copy-start | bytes 3076
  268.4 304.2 %all-reduce.18.cloned.1.call-start = ((), (), s32[]{:S(2)}) async-start(), calls=%async_computation.4 | async-start | bytes 6291456 | tf_op jit(solution)/shard_map/psum | solution.py:236
  333.2 10.3 %copy-start.28 = (bf16[16,64,8,24]{1,3,2,0:T(8,128)(2,1)S(1)}, bf16[16,64,8,24]{1,3,2,0:T(8,128)(2,1)}, u32[]{:S(2)}) copy-start(bf16[16,64,8,24]{1,3,2,0:T(8,128)(2,1)} %fusion.115) | copy-start | bytes 1179652
  338.6 11.7 %copy-start.85 = (f32[3]{0:T(128)S(1)}, f32[3]{0:T(128)}, u32[]{:S(2)}) copy-start(f32[3]{0:T(128)} %constant.348.clone) | copy-start | bytes 40
  353.0 270.7 %all-reduce.16.cloned.1.call-start = ((), (), s32[]{:S(2)}) async-start(), calls=%async_computation.3 | async-start | bytes 3538944 | tf_op jit(solution)/shard_map/psum | solution.py:296
  361.3 9.2 %copy-start.23 = (bf16[1024,192]{0,1:T(8,128)(2,1)S(1)}, bf16[1024,192]{0,1:T(8,128)(2,1)}, u32[]{:S(2)}) copy-start(bf16[1024,192]{0,1:T(8,128)(2,1)} %reshape.250) | copy-start | bytes 1179652
  375.5 318.8 %all-reduce.14.cloned.1.call-start = ((), (), s32[]{:S(2)}) async-start(), calls=%async_computation.2 | async-start | bytes 131072 | tf_op jit(solution)/shard_map/psum | solution.py:304
  375.6 165.0 %copy-start.17 = (bf16[16,64,64,8]{1,2,3,0:T(8,128)(2,1)S(1)}, bf16[16,64,64,8]{1,2,3,0:T(8,128)(2,1)}, u32[]{:S(2)}) copy-start(bf16[16,64,64,8]{1,2,3,0:T(8,128)(2,1)} %get-tuple-element.374) | copy-start | bytes 3145732
  375.6 20.7 %copy-start.83 = (f32[1,128]{1,0:T(1,128)}, f32[1,128]{1,0:T(1,128)S(1)}, u32[]{:S(2)}) copy-start(f32[1,128]{1,0:T(1,128)S(1)} %get-tuple-element.602) | copy-start | bytes 1540 | tf_op jit(solution)/shard_map/while
  376.8 19.5 %copy-start.22 = (bf16[4,16384,8]{1,2,0:T(8,128)(2,1)S(1)}, bf16[4,16384,8]{1,2,0:T(8,128)(2,1)}, u32[]{:S(2)}) copy-start(bf16[4,16384,8]{1,2,0:T(8,128)(2,1)} %get-tuple-element.600) | copy-start | bytes 3145732 | tf_op jit(solution)/shard_map/while
  408.9 8.0 %copy-start.84 = (f32[1,128]{1,0:T(1,128)S(1)}, f32[1,128]{1,0:T(1,128)}, u32[]{:S(2)}) copy-start(f32[1,128]{1,0:T(1,128)} %copy-done.83) | copy-start | bytes 1540 | tf_op jit(solution)/shard_map/while
  416.9 20.5 %copy-start.83 = (f32[1,128]{1,0:T(1,128)}, f32[1,128]{1,0:T(1,128)S(1)}, u32[]{:S(2)}) copy-start(f32[1,128]{1,0:T(1,128)S(1)} %get-tuple-element.602) | copy-start | bytes 1540 | tf_op jit(solution)/shard_map/while
  418.0 19.5 %copy-start.22 = (bf16[4,16384,8]{1,2,0:T(8,128)(2,1)S(1)}, bf16[4,16384,8]{1,2,0:T(8,128)(2,1)}, u32[]{:S(2)}) copy-start(bf16[4,16384,8]{1,2,0:T(8,128)(2,1)} %get-tuple-element.600) | copy-start | bytes 3145732 | tf_op jit(solution)/shard_map/while
  450.0 8.0 %copy-start.84 = (f32[1,128]{1,0:T(1,128)S(1)}, f32[1,128]{1,0:T(1,128)}, u32[]{:S(2)}) copy-start(f32[1,128]{1,0:T(1,128)} %copy-done.83) | copy-start | bytes 1540 | tf_op jit(solution)/shard_map/while
  458.1 20.5 %copy-start.83 = (f32[1,128]{1,0:T(1,128)}, f32[1,128]{1,0:T(1,128)S(1)}, u32[]{:S(2)}) copy-start(f32[1,128]{1,0:T(1,128)S(1)} %get-tuple-element.602) | copy-start | bytes 1540 | tf_op jit(solution)/shard_map/while
  459.1 19.5 %copy-start.22 = (bf16[4,16384,8]{1,2,0:T(8,128)(2,1)S(1)}, bf16[4,16384,8]{1,2,0:T(8,128)(2,1)}, u32[]{:S(2)}) copy-start(bf16[4,16384,8]{1,2,0:T(8,128)(2,1)} %get-tuple-element.600) | copy-start | bytes 3145732 | tf_op jit(solution)/shard_map/while
  491.2 8.0 %copy-start.84 = (f32[1,128]{1,0:T(1,128)S(1)}, f32[1,128]{1,0:T(1,128)}, u32[]{:S(2)}) copy-start(f32[1,128]{1,0:T(1,128)} %copy-done.83) | copy-start | bytes 1540 | tf_op jit(solution)/shard_map/while
  499.2 20.5 %copy-start.83 = (f32[1,128]{1,0:T(1,128)}, f32[1,128]{1,0:T(1,128)S(1)}, u32[]{:S(2)}) copy-start(f32[1,128]{1,0:T(1,128)S(1)} %get-tuple-element.602) | copy-start | bytes 1540 | tf_op jit(solution)/shard_map/while
  500.3 19.5 %copy-start.22 = (bf16[4,16384,8]{1,2,0:T(8,128)(2,1)S(1)}, bf16[4,16384,8]{1,2,0:T(8,128)(2,1)}, u32[]{:S(2)}) copy-start(bf16[4,16384,8]{1,2,0:T(8,128)(2,1)} %get-tuple-element.600) | copy-start | bytes 3145732 | tf_op jit(solution)/shard_map/while
  549.8 21.5 %copy-start.67 = (f32[256]{0:T(256)S(1)}, f32[256]{0:T(256)}, u32[]{:S(2)}) copy-start(f32[256]{0:T(256)} %copy-done.66) | copy-start | bytes 3076
  549.8 21.5 %copy-start.72 = (f32[256]{0:T(256)S(1)}, f32[256]{0:T(256)}, u32[]{:S(2)}) copy-start(f32[256]{0:T(256)} %add_rsqrt_fusion) | copy-start | bytes 3076
  549.8 22.9 %copy-start.3 = (bf16[1024,768]{1,0:T(8,128)(2,1)S(1)}, bf16[1024,768]{1,0:T(8,128)(2,1)}, u32[]{:S(2)}) copy-start(bf16[1024,768]{1,0:T(8,128)(2,1)} %param.26) | copy-start | bytes 4718596
  549.8 22.9 %copy-start.42 = (f32[1024]{0:T(1024)S(1)}, f32[1024]{0:T(1024)}, u32[]{:S(2)}) copy-start(f32[1024]{0:T(1024)} %copy-done.40) | copy-start | bytes 12292
  549.8 22.9 %copy-start.49 = (f32[768]{0:T(1024)S(1)}, f32[768]{0:T(1024)}, u32[]{:S(2)}) copy-start(f32[768]{0:T(1024)} %param.31) | copy-start | bytes 9220
  578.4 117.4 %copy-start.1 = (bf16[3,768,192]{1,2,0:T(8,128)(2,1)S(1)}, bf16[3,768,192]{1,2,0:T(8,128)(2,1)}, u32[]{:S(2)}) copy-start(bf16[3,768,192]{1,2,0:T(8,128)(2,1)} %param.27) | copy-start | bytes 2654212
  (81 other events, 310.0 us)
Sparse Core Ops, SparseCore 0:
  206.7 44.8 all-reduce.9
  268.6 42.8 all-reduce.11
  353.2 68.3 all-reduce.17
  425.9 94.4 all-reduce.15
  572.7 121.4 all-reduce.13
where the time goes:
time: 708 us; the launch traced here: 702 us
  matrix products  279 us (39%)
  waiting for transfers between devices  139 us (20%)
  local copies, waits for them, and re-layouts  115 us (16%)
  other arithmetic  94.3 us (13%)
  blocking collectives  58.9 us (8%)
  between operations  15 us (2%)
    dot_general x4, matrix products, one_block(): return jnp.dot(hidden, kernel_w2, preferred_element_type=jnp.float32)  84.6 us
    dot_general x4, matrix products, one_block(): inner = jnp.dot(basis_b, kernel_w1, preferred_element_type=jnp.float32)  77.8 us
    psum x1, waiting for transfers between devices, body(): lax.psum((grad_kw1, grad_cen, grad_wid, grad_g1, grad_b1, grad_g2, grad_b...  62.5 us
    dynamic_update_slice x8, local copies, waits for them, and re-layouts, kernel_geo(): result = lax.map(one_block, dist_rows.reshape(total // block, block))  44.1 us
    psum x1, blocking collectives, body(): lax.psum((grad_kw1, grad_cen, grad_wid, grad_g1, grad_b1, grad_g2, grad_b...  40.9 us
    psum x1, waiting for transfers between devices, body(): lax.psum(attn_part.astype(jnp.bfloat16), 'tensor').astype(jnp.float32)  39.8 us
    psum x1, waiting for transfers between devices, body(): lax.psum(two_part.astype(jnp.bfloat16), 'tensor').astype(jnp.float32)  36.9 us
    reduce_sum x4, other arithmetic, kernels(): offset = (place - centers) / widths  29.6 us
  transfers between devices with their start and end apart: 5, of which 3 were waited for; matrix products, arithmetic and copies ran while one was open for 32% of the time, Pallas kernels for 0%

commit v1 on v0

--- a/solution.py
+++ b/solution.py
@@ -1,3 +1,4 @@
+import functools
 from functools import partial
 import math
 import jax
@@ -9,6 +10,14 @@
 eps = 1e-05
 neg_fill = -1000000000.0
 highest = lax.Precision.HIGHEST
+
+
+def view_match(row_data, across):
+    found_now = lax.all_gather(row_data, across)
+    return jnp.sum(found_now, axis=0)
+
+
+hold_numbers = functools.partial(view_match, across="dp")
 
 
 def norm_rows(values, gain, shift):
@@ -297,7 +306,7 @@
         lax.psum(grad_out.astype(jnp.bfloat16), "dp").astype(jnp.float32),
         lax.psum(grad_ff1.astype(jnp.bfloat16), "dp").astype(jnp.float32),
         lax.psum(grad_ff2.astype(jnp.bfloat16), "dp").astype(jnp.float32),
-        lax.psum(grad_spd.astype(jnp.bfloat16), "dp").astype(jnp.float32),
+        hold_numbers(grad_spd.astype(jnp.bfloat16)).astype(jnp.float32),
         lax.psum(grad_edge.astype(jnp.bfloat16), "dp").astype(jnp.float32),
         lax.psum(grad_kw2.astype(jnp.bfloat16), "dp").astype(jnp.float32),
     )

time: 708 us -> 732 us (1.034)
  blocking collectives: 58.9 us -> 83.3 us
    all_gather x0 -> x1, blocking collectives: none -> 21.6 us  [view_match(): found_now = lax.all_gather(row_data, across)]
  transfers between devices with their start and end apart: 5 -> 5, of which waited for: 3 -> 3; matrix products, arithmetic and copies ran while one was open for 32% -> 31% of each run, Pallas kernels for 0% -> 0%
where the time goes in v1:
time: 732 us; the launch traced here: 727 us
  matrix products  279 us (38%)
  waiting for transfers between devices  139 us (19%)
  local copies, waits for them, and re-layouts  115 us (16%)
  other arithmetic  94.5 us (13%)
  blocking collectives  83.3 us (11%)
  between operations  15 us (2%)
    dot_general x4, matrix products, one_block(): return jnp.dot(hidden, kernel_w2, preferred_element_type=jnp.float32)  84.6 us
    dot_general x4, matrix products, one_block(): inner = jnp.dot(basis_b, kernel_w1, preferred_element_type=jnp.float32)  77.8 us
    psum x1, waiting for transfers between devices, body(): lax.psum((grad_kw1, grad_cen, grad_wid, grad_g1, grad_b1, grad_g2, grad_b...  62.6 us
    psum x1, blocking collectives, body(): lax.psum((grad_kw1, grad_cen, grad_wid, grad_g1, grad_b1, grad_g2, grad_b...  44.7 us
    dynamic_update_slice x8, local copies, waits for them, and re-layouts, kernel_geo(): result = lax.map(one_block, dist_rows.reshape(total // block, block))  44.4 us
    psum x1, waiting for transfers between devices, body(): lax.psum(attn_part.astype(jnp.bfloat16), 'tensor').astype(jnp.float32)  39.7 us
    psum x1, waiting for transfers between devices, body(): lax.psum(two_part.astype(jnp.bfloat16), 'tensor').astype(jnp.float32)  36.9 us
    reduce_sum x4, other arithmetic, kernels(): offset = (place - centers) / widths  29.6 us
  transfers between devices with their start and end apart: 5, of which 3 were waited for; matrix products, arithmetic and copies ran while one was open for 31% of the time, Pallas kernels for 0%

profile of v1, /device:TPU:1, one launch (start us, length us, event | category | flops | bytes accessed | tf_op | source)
XLA Modules:
  0.0 727.0 jit_solution(6240090821915042095)
XLA Ops:
  17.9 129.5 %while.6 = (s32[]{:T(128)}, f32[4,16384,8]{1,0,2:T(4,128)}, s32[4,16384]{1,0:T(4,128)S(1)}, f32[128]{0:T(128)S(1)}, f32[128]{0:T(128)S(1)}, /*index=5*/bf16[128,...) while((s32[]{:T(128)}, f32[4,16384,8]{1,0,2:T(4,128)}, s32[4,16384]{1,0:T(4,128)S(1)}, ...), condition=%wide.region_3.4_spmd, body=%wide.region_2.3_spmd.sunk | while | flops 719355904 | bytes 2853997 | solution.py:50
  18.2 21.2 %convolution_bitcast_fusion.2 = f32[1,16384,8]{1,2,0:T(8,128)S(1)} fusion(bf16[128,8]{0,1:T(8,128)(2,1)S(1)} %get-tuple-element.571, bf16[128,128]{1,0:T(8,128)(2,1)S(1)} %get-tuple-element.570, f32[128]{0:T(128)S(1)} %get-tuple-element.569, f32[128]{0:T(128)S(1)} %get-tuple-element.568, f32[16384]{0:T(1024)S(1)} %bitcast.184), kind=kOutput, calls=%fused_computation.clone.1 | convolution fusion | flops 719323136 | bytes 625664 | tf_op jit(solution)/shard_map/while/body/eval_jaxpr/dot_general | solution.py:48
  39.9 10.5 %dynamic_update_slice.20 = f32[4,16384,8]{1,0,2:T(4,128)} dynamic-update-slice(f32[4,16384,8]{1,0,2:T(4,128)} %get-tuple-element.557, f32[1,16384,8]{1,0,2:T(1,128)S(1)} %copy.156, s32[]{:T(128)S(6)} %copy.160, s32[]{:T(128)} %constant.312.clone.1..sunk, s32[]{:T(128)} %constant.312.clone.1..sunk) | dynamic-update-slice | bytes 1048580 | tf_op jit(solution)/shard_map/while/body/jit(dynamic_update_index_in_dim)/dynamic_update_slice | solution.py:50
  50.5 21.2 %convolution_bitcast_fusion.2 = f32[1,16384,8]{1,2,0:T(8,128)S(1)} fusion(bf16[128,8]{0,1:T(8,128)(2,1)S(1)} %get-tuple-element.571, bf16[128,128]{1,0:T(8,128)(2,1)S(1)} %get-tuple-element.570, f32[128]{0:T(128)S(1)} %get-tuple-element.569, f32[128]{0:T(128)S(1)} %get-tuple-element.568, f32[16384]{0:T(1024)S(1)} %bitcast.184), kind=kOutput, calls=%fused_computation.clone.1 | convolution fusion | flops 719323136 | bytes 625664 | tf_op jit(solution)/shard_map/while/body/eval_jaxpr/dot_general | solution.py:48
  72.2 10.5 %dynamic_update_slice.20 = f32[4,16384,8]{1,0,2:T(4,128)} dynamic-update-slice(f32[4,16384,8]{1,0,2:T(4,128)} %get-tuple-element.557, f32[1,16384,8]{1,0,2:T(1,128)S(1)} %copy.156, s32[]{:T(128)S(6)} %copy.160, s32[]{:T(128)} %constant.312.clone.1..sunk, s32[]{:T(128)} %constant.312.clone.1..sunk) | dynamic-update-slice | bytes 1048580 | tf_op jit(solution)/shard_map/while/body/jit(dynamic_update_index_in_dim)/dynamic_update_slice | solution.py:50
  82.9 21.2 %convolution_bitcast_fusion.2 = f32[1,16384,8]{1,2,0:T(8,128)S(1)} fusion(bf16[128,8]{0,1:T(8,128)(2,1)S(1)} %get-tuple-element.571, bf16[128,128]{1,0:T(8,128)(2,1)S(1)} %get-tuple-element.570, f32[128]{0:T(128)S(1)} %get-tuple-element.569, f32[128]{0:T(128)S(1)} %get-tuple-element.568, f32[16384]{0:T(1024)S(1)} %bitcast.184), kind=kOutput, calls=%fused_computation.clone.1 | convolution fusion | flops 719323136 | bytes 625664 | tf_op jit(solution)/shard_map/while/body/eval_jaxpr/dot_general | solution.py:48
  104.6 10.5 %dynamic_update_slice.20 = f32[4,16384,8]{1,0,2:T(4,128)} dynamic-update-slice(f32[4,16384,8]{1,0,2:T(4,128)} %get-tuple-element.557, f32[1,16384,8]{1,0,2:T(1,128)S(1)} %copy.156, s32[]{:T(128)S(6)} %copy.160, s32[]{:T(128)} %constant.312.clone.1..sunk, s32[]{:T(128)} %constant.312.clone.1..sunk) | dynamic-update-slice | bytes 1048580 | tf_op jit(solution)/shard_map/while/body/jit(dynamic_update_index_in_dim)/dynamic_update_slice | solution.py:50
  115.2 21.2 %convolution_bitcast_fusion.2 = f32[1,16384,8]{1,2,0:T(8,128)S(1)} fusion(bf16[128,8]{0,1:T(8,128)(2,1)S(1)} %get-tuple-element.571, bf16[128,128]{1,0:T(8,128)(2,1)S(1)} %get-tuple-element.570, f32[128]{0:T(128)S(1)} %get-tuple-element.569, f32[128]{0:T(128)S(1)} %get-tuple-element.568, f32[16384]{0:T(1024)S(1)} %bitcast.184), kind=kOutput, calls=%fused_computation.clone.1 | convolution fusion | flops 719323136 | bytes 625664 | tf_op jit(solution)/shard_map/while/body/eval_jaxpr/dot_general | solution.py:48
  136.9 10.5 %dynamic_update_slice.20 = f32[4,16384,8]{1,0,2:T(4,128)} dynamic-update-slice(f32[4,16384,8]{1,0,2:T(4,128)} %get-tuple-element.557, f32[1,16384,8]{1,0,2:T(1,128)S(1)} %copy.156, s32[]{:T(128)S(6)} %copy.160, s32[]{:T(128)} %constant.312.clone.1..sunk, s32[]{:T(128)} %constant.312.clone.1..sunk) | dynamic-update-slice | bytes 1048580 | tf_op jit(solution)/shard_map/while/body/jit(dynamic_update_index_in_dim)/dynamic_update_slice | solution.py:50
  148.1 5.0 squeeze.56
  153.1 5.5 copy.83
  163.5 7.7 %fusion.83 = f32[16,64,64,8]{2,3,1,0:T(8,128)} fusion(s32[16,64,64]{2,1,0:T(8,128)} %param.43, f32[32,8]{0,1:T(8,128)S(1)} %copy-done.68), kind=kOutput, calls=%fused_computation.114 | convolution fusion | flops 203423744 | bytes 2360320 | tf_op jit(solution)/shard_map/while/body/eval_jaxpr/dot_general | solution.py:96
  171.3 5.4 copy.80
  176.7 7.5 %fusion.82 = f32[16,64,64,8]{2,3,1,0:T(8,128)} fusion(s32[16,64,64]{2,1,0:T(8,128)} %param.44, f32[32,8]{0,1:T(8,128)S(1)} %copy-done.69), kind=kOutput, calls=%fused_computation.112 | convolution fusion | flops 203423744 | bytes 2360320 | tf_op jit(solution)/shard_map/while/body/eval_jaxpr/dot_general | solution.py:96
  184.2 5.4 copy.81
  189.6 8.2 %fusion.154 = (f32[16,8,64]{2,1,0:T(8,128)S(1)}, f32[16,8,64,64]{2,3,1,0:T(8,128)S(1)}, f32[16,64,64,8]{1,2,3,0:T(8,128)}, f32[16,8,64,64]{2,3,1,0:T(8,128)}) fusion(pred[16,64]{1,0:T(8,128)(4,1)S(1)} %copy-done.61, f32[16,64,64,8]{1,2,3,0:T(8,128)} %copy.83, f32[16]{0:T(128)S(1)} %copy-done.75, f32[16,64,64,8]{1,2,3,0:T(8,128)} %copy.80, ...), kind=kOutput, calls=%fused_computation.249 | convolution fusion | flops 28827648 | bytes 13403264 | tf_op jit(solution)/shard_map/while/body/eval_jaxpr/bihe,bjhe->bhij/dot_general | solution.py:106
  212.1 39.7 %all-reduce.10.cloned.1.call-done = bf16[1024,768]{1,0:T(8,128)(2,1)} async-done(((bf16[1024,768]{1,0:T(8,128)(2,1)}), bf16[1024,768]{1,0:T(8,128)(2,1)}) %all-reduce.10.cloned.1.call-update) | async-done | bytes 1572880 | tf_op jit(solution)/shard_map/psum | solution.py:239
  274.9 36.9 %all-reduce.12.cloned.1.call-done = bf16[1024,768]{1,0:T(8,128)(2,1)} async-done(((bf16[1024,768]{1,0:T(8,128)(2,1)}), bf16[1024,768]{1,0:T(8,128)(2,1)}) %all-reduce.12.cloned.1.call-update) | async-done | bytes 1572880 | tf_op jit(solution)/shard_map/psum | solution.py:253
  353.4 6.6 broadcast_multiply_fusion.1
  375.9 164.8 %while.7 = (s32[]{:T(128)}, f32[128,128]{1,0:T(8,128)S(1)}, f32[128,8]{0,1:T(8,128)S(1)}, f32[128]{0:T(128)}, f32[128]{0:T(128)}, /*index=5*/s32[4,16384]{1,0:T(...) while((s32[]{:T(128)}, f32[128,128]{1,0:T(8,128)S(1)}, ...), condition=%wide.region_40.41_spmd.clone, body=%wide.region_36.40_spmd.clone.sunk | while | flops 1914768128 | bytes 101811056 | solution.py:81
  377.1 19.5 %fusion.219 = (f32[16384,128]{1,0:T(8,128)S(1)}, f32[16384,128]{1,0:T(8,128)S(1)}) fusion(bf16[128,128]{1,0:T(8,128)(2,1)S(1)} %get-tuple-element.610, f32[128]{0:T(128)S(1)} %get-tuple-element.609, f32[128]{0:T(128)S(1)} %get-tuple-element.608, f32[16384]{0:T(1024)S(1)} %bitcast.177), kind=kOutput, calls=%fused_computation.69.clone.1 | convolution fusion | flops 679477248 | bytes 16876544 | tf_op jit(solution)/shard_map/while/body/eval_jaxpr/dot_general | solution.py:64
  409.2 7.4 %fusion.223 = (f32[128]{0:T(128)S(1)}, f32[128]{0:T(128)S(1)}, f32[128]{0:T(128)S(1)}) fusion(f32[16384,128]{1,0:T(8,128)S(1)} %get-tuple-element.540, f32[128]{0:T(128)S(1)} %divide_bitcast_fusion.2, f32[128]{0:T(128)S(1)} %get-tuple-element.608, f32[16384]{0:T(1024)S(1)} %bitcast.180, f32[128]{0:T(128)S(1)} %get-tuple-element.609, ...), kind=kLoop, calls=%fused_computation.66.clone.1 | loop fusion | flops 25165440 | bytes 16845824 | tf_op jit(solution)/shard_map/while/body/eval_jaxpr/transpose(jvp())/reduce_sum | solution.py:35
  418.2 19.5 %fusion.219 = (f32[16384,128]{1,0:T(8,128)S(1)}, f32[16384,128]{1,0:T(8,128)S(1)}) fusion(bf16[128,128]{1,0:T(8,128)(2,1)S(1)} %get-tuple-element.610, f32[128]{0:T(128)S(1)} %get-tuple-element.609, f32[128]{0:T(128)S(1)} %get-tuple-element.608, f32[16384]{0:T(1024)S(1)} %bitcast.177), kind=kOutput, calls=%fused_computation.69.clone.1 | convolution fusion | flops 679477248 | bytes 16876544 | tf_op jit(solution)/shard_map/while/body/eval_jaxpr/dot_general | solution.py:64
  450.3 7.4 %fusion.223 = (f32[128]{0:T(128)S(1)}, f32[128]{0:T(128)S(1)}, f32[128]{0:T(128)S(1)}) fusion(f32[16384,128]{1,0:T(8,128)S(1)} %get-tuple-element.540, f32[128]{0:T(128)S(1)} %divide_bitcast_fusion.2, f32[128]{0:T(128)S(1)} %get-tuple-element.608, f32[16384]{0:T(1024)S(1)} %bitcast.180, f32[128]{0:T(128)S(1)} %get-tuple-element.609, ...), kind=kLoop, calls=%fused_computation.66.clone.1 | loop fusion | flops 25165440 | bytes 16845824 | tf_op jit(solution)/shard_map/while/body/eval_jaxpr/transpose(jvp())/reduce_sum | solution.py:35
  459.3 19.5 %fusion.219 = (f32[16384,128]{1,0:T(8,128)S(1)}, f32[16384,128]{1,0:T(8,128)S(1)}) fusion(bf16[128,128]{1,0:T(8,128)(2,1)S(1)} %get-tuple-element.610, f32[128]{0:T(128)S(1)} %get-tuple-element.609, f32[128]{0:T(128)S(1)} %get-tuple-element.608, f32[16384]{0:T(1024)S(1)} %bitcast.177), kind=kOutput, calls=%fused_computation.69.clone.1 | convolution fusion | flops 679477248 | bytes 16876544 | tf_op jit(solution)/shard_map/while/body/eval_jaxpr/dot_general | solution.py:64
  491.4 7.4 %fusion.223 = (f32[128]{0:T(128)S(1)}, f32[128]{0:T(128)S(1)}, f32[128]{0:T(128)S(1)}) fusion(f32[16384,128]{1,0:T(8,128)S(1)} %get-tuple-element.540, f32[128]{0:T(128)S(1)} %divide_bitcast_fusion.2, f32[128]{0:T(128)S(1)} %get-tuple-element.608, f32[16384]{0:T(1024)S(1)} %bitcast.180, f32[128]{0:T(128)S(1)} %get-tuple-element.609, ...), kind=kLoop, calls=%fused_computation.66.clone.1 | loop fusion | flops 25165440 | bytes 16845824 | tf_op jit(solution)/shard_map/while/body/eval_jaxpr/transpose(jvp())/reduce_sum | solution.py:35
  500.5 19.5 %fusion.219 = (f32[16384,128]{1,0:T(8,128)S(1)}, f32[16384,128]{1,0:T(8,128)S(1)}) fusion(bf16[128,128]{1,0:T(8,128)(2,1)S(1)} %get-tuple-element.610, f32[128]{0:T(128)S(1)} %get-tuple-element.609, f32[128]{0:T(128)S(1)} %get-tuple-element.608, f32[16384]{0:T(1024)S(1)} %bitcast.177), kind=kOutput, calls=%fused_computation.69.clone.1 | convolution fusion | flops 679477248 | bytes 16876544 | tf_op jit(solution)/shard_map/while/body/eval_jaxpr/dot_general | solution.py:64
  532.6 7.4 %fusion.223 = (f32[128]{0:T(128)S(1)}, f32[128]{0:T(128)S(1)}, f32[128]{0:T(128)S(1)}) fusion(f32[16384,128]{1,0:T(8,128)S(1)} %get-tuple-element.540, f32[128]{0:T(128)S(1)} %divide_bitcast_fusion.2, f32[128]{0:T(128)S(1)} %get-tuple-element.608, f32[16384]{0:T(1024)S(1)} %bitcast.180, f32[128]{0:T(128)S(1)} %get-tuple-element.609, ...), kind=kLoop, calls=%fused_computation.66.clone.1 | loop fusion | flops 25165440 | bytes 16845824 | tf_op jit(solution)/shard_map/while/body/eval_jaxpr/transpose(jvp())/reduce_sum | solution.py:35
  547.6 21.6 %all-gather.1 = bf16[8,32,8]{1,2,0:T(8,128)(2,1)S(1)} all-gather(bf16[1,32,8]{1,2,0:T(8,128)(2,1)S(1)} %fusion.124), channel_id=2, replica_groups=mesh['dp'=8,'tensor'=4] {'dp'}, dimensions={0}, use_global_device_ids=true | all-gather | bytes 4608 | tf_op jit(solution)/shard_map/all_gather | solution.py:16
  572.1 17.0 %all-reduce.1 = (bf16[32,8]{0,1:T(8,128)(2,1)S(1)}, bf16[128,8]{0,1:T(8,128)(2,1)S(1)}) all-reduce(bf16[32,8]{0,1:T(8,128)(2,1)S(1)} %fusion.123, bf16[128,8]{0,1:T(8,128)(2,1)S(1)} %convert_element_type.294), channel_id=1, replica_groups=mesh['dp'=8,'tensor'=4] {'dp'}, use_global_device_ids=true, to_apply=%region_35.36 | all-reduce | flops 1280 | bytes 5120 | tf_op jit(solution)/shard_map/psum | solution.py:310
  603.6 44.7 %all-reduce = (f32[768]{0:T(1024)}, f32[768]{0:T(1024)}, f32[768]{0:T(1024)}, f32[768]{0:T(1024)}, f32[128]{0:T(128)}, /*index=5*/f32[128]{0:T(128)}) all-reduce(f32[768]{0:T(1024)S(1)} %get-tuple-element.332, f32[768]{0:T(1024)S(1)} %get-tuple-element.331, ...), channel_id=1, replica_groups=mesh['dp'=8,'tensor'=4] {'dp','tensor'}, use_global_device_ids=true, to_apply=%region_25.26 | all-reduce | flops 3328 | bytes 26624 | tf_op jit(solution)/shard_map/psum | solution.py:313
  656.3 62.6 %all-reduce.14.cloned.1.call-done = f32[128,128]{1,0:T(8,128)} async-done(((f32[128,128]{1,0:T(8,128)}), f32[128,128]{1,0:T(8,128)}) %all-reduce.14.cloned.1.call-update) | async-done | bytes 65552 | tf_op jit(solution)/shard_map/psum | solution.py:313
  (361 shorter events, 203.1 us)
Async XLA Ops:
  7.2 244.6 %all-reduce.10.cloned.1.call-start = ((), (), s32[]{:S(2)}) async-start(), calls=%async_computation | async-start | bytes 3145728 | tf_op jit(solution)/shard_map/psum | solution.py:239
  160.0 39.1 %copy-start.26 = (bf16[16,64,8,24]{1,0,3,2:T(8,128)(2,1)}, bf16[16,64,8,24]{1,0,3,2:T(8,128)(2,1)S(1)}, u32[]{:S(2)}) copy-start(bf16[16,64,8,24]{1,0,3,2:T(8,128)(2,1)S(1)} %convert_element_type.241) | copy-start | bytes 1179652
  163.5 26.0 %copy-start.18 = (bf16[16,64,8,24]{1,0,3,2:T(8,128)(2,1)}, bf16[16,64,8,24]{1,0,3,2:T(8,128)(2,1)S(1)}, u32[]{:S(2)}) copy-start(bf16[16,64,8,24]{1,0,3,2:T(8,128)(2,1)S(1)} %convert_element_type.244) | copy-start | bytes 1179652
  206.8 105.0 %all-reduce.12.cloned.1.call-start = ((), (), s32[]{:S(2)}) async-start(), calls=%async_computation.1 | async-start | bytes 3145728 | tf_op jit(solution)/shard_map/psum | solution.py:253
  210.1 46.1 %copy-start.64 = (f32[256]{0:T(256)}, f32[256]{0:T(256)S(1)}, u32[]{:S(2)}) copy-start(f32[256]{0:T(256)S(1)} %broadcast_multiply_fusion.5) | copy-start | bytes 3076
  212.1 44.2 %copy-start.45 = (f32[768]{0:T(1024)S(1)}, f32[768]{0:T(1024)}, u32[]{:S(2)}) copy-start(f32[768]{0:T(1024)} %param.33) | copy-start | bytes 9220
  212.1 44.2 %copy-start.70 = (f32[768]{0:T(1024)S(1)}, f32[768]{0:T(1024)}, u32[]{:S(2)}) copy-start(f32[768]{0:T(1024)} %param.34) | copy-start | bytes 9220
  265.1 9.8 %copy-start.66 = (f32[256]{0:T(256)}, f32[256]{0:T(256)S(1)}, u32[]{:S(2)}) copy-start(f32[256]{0:T(256)S(1)} %broadcast_multiply_fusion.4) | copy-start | bytes 3076
  268.7 324.7 %all-reduce.18.cloned.1.call-start = ((), (), s32[]{:S(2)}) async-start(), calls=%async_computation.4 | async-start | bytes 6291456 | tf_op jit(solution)/shard_map/psum | solution.py:245
  333.5 10.3 %copy-start.28 = (bf16[16,64,8,24]{1,3,2,0:T(8,128)(2,1)S(1)}, bf16[16,64,8,24]{1,3,2,0:T(8,128)(2,1)}, u32[]{:S(2)}) copy-start(bf16[16,64,8,24]{1,3,2,0:T(8,128)(2,1)} %fusion.115) | copy-start | bytes 1179652
  338.9 11.7 %copy-start.86 = (f32[3]{0:T(128)S(1)}, f32[3]{0:T(128)}, u32[]{:S(2)}) copy-start(f32[3]{0:T(128)} %constant.350.clone) | copy-start | bytes 40
  353.3 295.0 %all-reduce.16.cloned.1.call-start = ((), (), s32[]{:S(2)}) async-start(), calls=%async_computation.3 | async-start | bytes 3538944 | tf_op jit(solution)/shard_map/psum | solution.py:305
  361.6 9.2 %copy-start.23 = (bf16[1024,192]{0,1:T(8,128)(2,1)S(1)}, bf16[1024,192]{0,1:T(8,128)(2,1)}, u32[]{:S(2)}) copy-start(bf16[1024,192]{0,1:T(8,128)(2,1)} %reshape.250) | copy-start | bytes 1179652
  375.8 343.1 %all-reduce.14.cloned.1.call-start = ((), (), s32[]{:S(2)}) async-start(), calls=%async_computation.2 | async-start | bytes 131072 | tf_op jit(solution)/shard_map/psum | solution.py:313
  375.8 164.9 %copy-start.17 = (bf16[16,64,64,8]{1,2,3,0:T(8,128)(2,1)S(1)}, bf16[16,64,64,8]{1,2,3,0:T(8,128)(2,1)}, u32[]{:S(2)}) copy-start(bf16[16,64,64,8]{1,2,3,0:T(8,128)(2,1)} %get-tuple-element.385) | copy-start | bytes 3145732
  375.9 20.7 %copy-start.84 = (f32[1,128]{1,0:T(1,128)}, f32[1,128]{1,0:T(1,128)S(1)}, u32[]{:S(2)}) copy-start(f32[1,128]{1,0:T(1,128)S(1)} %get-tuple-element.613) | copy-start | bytes 1540 | tf_op jit(solution)/shard_map/while
  377.1 19.5 %copy-start.22 = (bf16[4,16384,8]{1,2,0:T(8,128)(2,1)S(1)}, bf16[4,16384,8]{1,2,0:T(8,128)(2,1)}, u32[]{:S(2)}) copy-start(bf16[4,16384,8]{1,2,0:T(8,128)(2,1)} %get-tuple-element.611) | copy-start | bytes 3145732 | tf_op jit(solution)/shard_map/while
  417.2 20.5 %copy-start.84 = (f32[1,128]{1,0:T(1,128)}, f32[1,128]{1,0:T(1,128)S(1)}, u32[]{:S(2)}) copy-start(f32[1,128]{1,0:T(1,128)S(1)} %get-tuple-element.613) | copy-start | bytes 1540 | tf_op jit(solution)/shard_map/while
  418.2 19.5 %copy-start.22 = (bf16[4,16384,8]{1,2,0:T(8,128)(2,1)S(1)}, bf16[4,16384,8]{1,2,0:T(8,128)(2,1)}, u32[]{:S(2)}) copy-start(bf16[4,16384,8]{1,2,0:T(8,128)(2,1)} %get-tuple-element.611) | copy-start | bytes 3145732 | tf_op jit(solution)/shard_map/while
  450.3 8.0 %copy-start.85 = (f32[1,128]{1,0:T(1,128)S(1)}, f32[1,128]{1,0:T(1,128)}, u32[]{:S(2)}) copy-start(f32[1,128]{1,0:T(1,128)} %copy-done.84) | copy-start | bytes 1540 | tf_op jit(solution)/shard_map/while
  458.3 20.5 %copy-start.84 = (f32[1,128]{1,0:T(1,128)}, f32[1,128]{1,0:T(1,128)S(1)}, u32[]{:S(2)}) copy-start(f32[1,128]{1,0:T(1,128)S(1)} %get-tuple-element.613) | copy-start | bytes 1540 | tf_op jit(solution)/shard_map/while
  459.3 19.5 %copy-start.22 = (bf16[4,16384,8]{1,2,0:T(8,128)(2,1)S(1)}, bf16[4,16384,8]{1,2,0:T(8,128)(2,1)}, u32[]{:S(2)}) copy-start(bf16[4,16384,8]{1,2,0:T(8,128)(2,1)} %get-tuple-element.611) | copy-start | bytes 3145732 | tf_op jit(solution)/shard_map/while
  499.4 20.5 %copy-start.84 = (f32[1,128]{1,0:T(1,128)}, f32[1,128]{1,0:T(1,128)S(1)}, u32[]{:S(2)}) copy-start(f32[1,128]{1,0:T(1,128)S(1)} %get-tuple-element.613) | copy-start | bytes 1540 | tf_op jit(solution)/shard_map/while
  500.4 19.5 %copy-start.22 = (bf16[4,16384,8]{1,2,0:T(8,128)(2,1)S(1)}, bf16[4,16384,8]{1,2,0:T(8,128)(2,1)}, u32[]{:S(2)}) copy-start(bf16[4,16384,8]{1,2,0:T(8,128)(2,1)} %get-tuple-element.611) | copy-start | bytes 3145732 | tf_op jit(solution)/shard_map/while
  543.6 26.2 %copy-start.30 = (bf16[16,64,64,8]{2,3,1,0:T(8,128)(2,1)S(1)}, bf16[16,64,64,8]{2,3,1,0:T(8,128)(2,1)}, u32[]{:S(2)}) copy-start(bf16[16,64,64,8]{2,3,1,0:T(8,128)(2,1)} %copy.98) | copy-start | bytes 3145732
  543.6 26.2 %copy-start.32 = (s32[16,64,64]{2,1,0:T(8,128)S(1)}, s32[16,64,64]{2,1,0:T(8,128)}, u32[]{:S(2)}) copy-start(s32[16,64,64]{2,1,0:T(8,128)} %param.44) | copy-start | bytes 786436
  572.1 19.9 %copy-start.67 = (f32[256]{0:T(256)S(1)}, f32[256]{0:T(256)}, u32[]{:S(2)}) copy-start(f32[256]{0:T(256)} %copy-done.66) | copy-start | bytes 3076
  572.1 19.9 %copy-start.72 = (f32[256]{0:T(256)S(1)}, f32[256]{0:T(256)}, u32[]{:S(2)}) copy-start(f32[256]{0:T(256)} %add_rsqrt_fusion) | copy-start | bytes 3076
  572.1 21.3 %copy-start.3 = (bf16[1024,768]{1,0:T(8,128)(2,1)S(1)}, bf16[1024,768]{1,0:T(8,128)(2,1)}, u32[]{:S(2)}) copy-start(bf16[1024,768]{1,0:T(8,128)(2,1)} %param.26) | copy-start | bytes 4718596
  572.1 21.3 %copy-start.42 = (f32[1024]{0:T(1024)S(1)}, f32[1024]{0:T(1024)}, u32[]{:S(2)}) copy-start(f32[1024]{0:T(1024)} %copy-done.40) | copy-start | bytes 12292
  572.1 21.3 %copy-start.49 = (f32[768]{0:T(1024)S(1)}, f32[768]{0:T(1024)}, u32[]{:S(2)}) copy-start(f32[768]{0:T(1024)} %param.31) | copy-start | bytes 9220
  599.1 121.2 %copy-start.1 = (bf16[3,768,192]{1,2,0:T(8,128)(2,1)S(1)}, bf16[3,768,192]{1,2,0:T(8,128)(2,1)}, u32[]{:S(2)}) copy-start(bf16[3,768,192]{1,2,0:T(8,128)(2,1)} %param.27) | copy-start | bytes 2654212
  (81 other events, 312.1 us)
Sparse Core Ops, SparseCore 0:
  206.9 44.8 all-reduce.9
  268.9 42.8 all-reduce.11
  353.5 68.3 all-reduce.17
  426.2 94.4 all-reduce.15
  593.5 125.2 all-reduce.13
